TPU v7x, 512 devices: a whole 4x4x16 slice. The times are simulated.
512 devices in a mesh: rows: 128 (over z, x, core), grp: 4 (over y).
Axes of the slice: x: 4, y: 4, z: 16, core: 2. Of those that a mesh axis runs over, the one named last changes fastest.
Arguments:
- features: bfloat16 [4, 196608, 128], P('grp', 'rows'), may hold values from -6 to 6
- length_scale: bfloat16 [4, 196608], P('grp', 'rows'), may hold values from 32 to 256
- prior: bfloat16 [4, 196608], P('grp', 'rows'), may hold values from 0.45 to 18
- partners: int32 [4, 1536, 16], P('grp', 'rows'), may hold values from 0 to 1535, as said below
- counts: int32 [4, 1536], P('grp', 'rows'), may hold values from 12 to 16
- projection: bfloat16 [128, 64], replicated, may hold values from -0.5 to 0.5
Outputs:
- first_basis: float32 [4, 64, 196608], P('grp', None, 'rows')
- embedding: float32 [4, 64, 196608], P('grp', None, 'rows')
Inputs may be any that keep to these rules, and one draw needn't show every extreme that they name: `partners`: slot 0 of each tile names the tile itself; slots 1 to 12 name tiles held by the same device; slots 13 onward name tiles held by other devices along rows in the same group. Tiles may repeat in a list. Over one device's tiles, slots 13 onward name tiles of any one other device at most 1 times, and exactly 1 times for some device.
All inputs are finite; a program needn't handle non-finite values.
Results may differ from a plain program's by a relative error of at most 0.0047.
Values may be sent and summed in bfloat16 or wider, within the bound.
A program may use at most 128 MiB of HBM per device.

v0:
```python
import jax
import jax.numpy as jnp
from jax import lax
from jax.sharding import PartitionSpec as P

NEAR = 13


def kernel_tiles(own_rows, own_norm, own_band, part_rows, part_norm, part_band, alive_mask):
    cross_products = jnp.einsum(
        "naf,nsbf->nsab", own_rows, part_rows, preferred_element_type=jnp.float32
    )
    distance = jnp.maximum(
        own_norm[:, None, :, None] + part_norm[:, :, None, :] - 2.0 * cross_products, 0.0
    )
    spread = (
        own_band.astype(jnp.float32)[:, None, :, None]
        + part_band.astype(jnp.float32)[:, :, None, :]
    )
    return jnp.where(alive_mask[:, :, None, None], jnp.exp(-distance / spread), 0.0)


def density_term(kernel, extras):
    return jnp.sum(kernel, axis=(1, 3))


def walk_term(kernel, extras):
    rounded = lax.optimization_barrier(kernel.astype(jnp.bfloat16))
    degree = jnp.sum(rounded.astype(jnp.float32) * extras[0][:, :, None, :], axis=(1, 3))
    product = jnp.einsum("nsab,nscb->nca", rounded, extras[1], preferred_element_type=jnp.float32)
    return (degree, product)


def apply_term(kernel, extras):
    rounded = kernel.astype(jnp.bfloat16)
    return jnp.einsum("nsab,nscb->nca", rounded, extras[0], preferred_element_type=jnp.float32)


def sweep_blocks(block_term, own_arrays, pool_arrays, slot_table, alive_table, block_size):
    tiles_dev = own_arrays[0].shape[0]

    def one_block(block_step):
        first_tile = block_step * block_size
        own_block = [
            lax.dynamic_slice_in_dim(member, first_tile, block_size, 0) for member in own_arrays
        ]
        slot_block = lax.dynamic_slice_in_dim(slot_table, first_tile, block_size, 0)
        alive_block = lax.dynamic_slice_in_dim(alive_table, first_tile, block_size, 0)
        gathered = [jnp.take(member, slot_block, axis=0) for member in pool_arrays]
        kernel = kernel_tiles(
            own_block[0],
            own_block[1],
            own_block[2],
            gathered[0],
            gathered[1],
            gathered[2],
            alive_block,
        )
        return block_term(kernel, gathered[3:])

    stacked = lax.map(one_block, jnp.arange(tiles_dev // block_size, dtype=jnp.int32))
    return jax.tree.map(
        lambda stacked_part: stacked_part.reshape((tiles_dev,) + stacked_part.shape[2:]), stacked
    )


def combined(
    block_term,
    own_arrays,
    near_extras,
    far_arrays,
    far_extras,
    near_table,
    far_table,
    alive_table,
    block_size,
):
    pool_arrays = tuple(
        (
            jnp.concatenate([near_member, far_member], axis=0)
            for near_member, far_member in zip(own_arrays + near_extras, far_arrays + far_extras)
        )
    )
    slot_table = jnp.concatenate([near_table, far_table + own_arrays[0].shape[0]], axis=1)
    return sweep_blocks(block_term, own_arrays, pool_arrays, slot_table, alive_table, block_size)


def orthonormal(raw_basis, total_rows):
    local_gram = jnp.einsum("nca,nda->cd", raw_basis, raw_basis, precision=lax.Precision.HIGHEST)
    gram_matrix = lax.psum(local_gram, ("rows", "grp")) / total_rows
    lower = jnp.linalg.cholesky(gram_matrix)
    identity = jnp.eye(gram_matrix.shape[0], dtype=jnp.float32)
    lower_inverse = lax.linalg.triangular_solve(lower, identity, left_side=True, lower=True)
    return jnp.einsum("dc,nca->nda", lower_inverse, raw_basis, precision=lax.Precision.HIGHEST)


def columns_first(tile_basis):
    return jnp.transpose(tile_basis, (1, 0, 2)).reshape(
        1, tile_basis.shape[1], tile_basis.shape[0] * tile_basis.shape[2]
    )


def shards(features, length_scale, prior, partners, counts, projection):
    tiles_dev = partners.shape[1]
    part_slots = partners.shape[2]
    tile_rows = features.shape[1] // tiles_dev
    feature_width = features.shape[2]
    column_count = projection.shape[1]
    nrows = lax.axis_size("rows")
    device_index = lax.axis_index("rows")
    own_rows = features[0].reshape(tiles_dev, tile_rows, feature_width)
    own_band = length_scale[0].reshape(tiles_dev, tile_rows)
    own_prior = prior[0].reshape(tiles_dev, tile_rows)
    own_norm = jnp.einsum("naf,naf->na", own_rows, own_rows, preferred_element_type=jnp.float32)
    partner_lists = partners[0]
    far_tiles = partner_lists[:, NEAR:].reshape(-1)
    far_count = far_tiles.shape[0]
    capacity = max(1, (3 * far_count + 2 * nrows - 3) // (2 * (nrows - 1)))
    near_table = partner_lists[:, :NEAR] - device_index * tiles_dev
    alive_table = jnp.arange(part_slots, dtype=jnp.int32)[None, :] < counts[0][:, None]
    block_size = 2
    owner_index = far_tiles // tiles_dev
    local_index = far_tiles % tiles_dev
    owner_hits = (owner_index[:, None] == jnp.arange(nrows, dtype=jnp.int32)[None, :]).astype(
        jnp.int32
    )
    slot_rank = jnp.sum((jnp.cumsum(owner_hits, axis=0) - owner_hits) * owner_hits, axis=1)
    wanted = jnp.zeros((nrows, capacity), jnp.int32).at[owner_index, slot_rank].set(local_index)
    requested = lax.all_to_all(wanted, "rows", split_axis=0, concat_axis=0, tiled=True)
    got_rows, got_band, got_prior = (
        lax.all_to_all(
            jnp.take(own_rows, requested, axis=0), "rows", split_axis=0, concat_axis=0, tiled=True
        ),
        lax.all_to_all(
            jnp.take(own_band, requested, axis=0), "rows", split_axis=0, concat_axis=0, tiled=True
        ),
        lax.all_to_all(
            jnp.take(own_prior, requested, axis=0), "rows", split_axis=0, concat_axis=0, tiled=True
        ),
    )
    far_rows = got_rows.reshape(nrows * capacity, tile_rows, feature_width)
    far_band = got_band.reshape(nrows * capacity, tile_rows)
    far_prior = got_prior.reshape(nrows * capacity, tile_rows)
    far_table = (owner_index * capacity + slot_rank).reshape(tiles_dev, part_slots - NEAR)
    far_norm = jnp.einsum("naf,naf->na", far_rows, far_rows, preferred_element_type=jnp.float32)
    own_arrays = (own_rows, own_norm, own_band)
    far_arrays = (far_rows, far_norm, far_band)
    density = combined(
        density_term, own_arrays, (), far_arrays, (), near_table, far_table, alive_table, block_size
    )
    own_inverse = 1.0 / density
    far_inverse = (
        lax.all_to_all(
            jnp.take(own_inverse, requested, axis=0).astype(jnp.bfloat16),
            "rows",
            split_axis=0,
            concat_axis=0,
            tiled=True,
        )
        .astype(jnp.float32)
        .reshape(nrows * capacity, tile_rows)
    )
    own_start = jnp.einsum("naf,fc->nca", own_rows, projection, preferred_element_type=jnp.float32)
    own_scaled = (own_start * (own_prior.astype(jnp.float32) * own_inverse)[:, None, :]).astype(
        jnp.bfloat16
    )
    far_start = jnp.einsum("naf,fc->nca", far_rows, projection, preferred_element_type=jnp.float32)
    far_scaled = (far_start * (far_prior.astype(jnp.float32) * far_inverse)[:, None, :]).astype(
        jnp.bfloat16
    )
    degree, product = combined(
        walk_term,
        own_arrays,
        (own_inverse, own_scaled),
        far_arrays,
        (far_inverse, far_scaled),
        near_table,
        far_table,
        alive_table,
        block_size,
    )
    total_rows = nrows * lax.axis_size("grp") * tiles_dev * tile_rows
    first_basis = orthonormal(product / degree[:, None, :], total_rows)
    own_next = (first_basis * own_inverse[:, None, :]).astype(jnp.bfloat16)
    far_next = lax.all_to_all(
        jnp.take(own_next, requested, axis=0), "rows", split_axis=0, concat_axis=0, tiled=True
    ).reshape(nrows * capacity, column_count, tile_rows)
    second = combined(
        apply_term,
        own_arrays,
        (own_next,),
        far_arrays,
        (far_next,),
        near_table,
        far_table,
        alive_table,
        block_size,
    )
    final_basis = orthonormal(second / degree[:, None, :], total_rows)
    return (columns_first(first_basis), columns_first(final_basis))


def solution(mesh):
    in_specs = (
        P("grp", "rows", None),
        P("grp", "rows"),
        P("grp", "rows"),
        P("grp", "rows", None),
        P("grp", "rows"),
        P(),
    )
    out_specs = (P("grp", None, "rows"), P("grp", None, "rows"))
    return jax.shard_map(shards, mesh=mesh, in_specs=in_specs, out_specs=out_specs, check_vma=False)
```

profile of v0, /device:TPU:1, one launch (start us, length us, event | category | flops | bytes accessed | tf_op | source)
XLA Modules:
  0.0 839.4 jit_solution(2037871099502354747)
XLA Ops:
  4.0 20.4 %all-to-all-start = ((s32[128,1,1]{2,1,0:T(1,128)}), s32[128,1,1]{2,1,0:T(1,128)S(1)}, u32[]{:S(2)}, u32[]{:S(2)}) async-start(s32[128,1,1]{2,1,0:T(1,128)} %copy.68), calls=%async_computation | async-start | bytes 131072 | tf_op jit(solution)/shard_map/all_to_all | solution.py:129
  25.8 13.4 %all-to-all-done = s32[128,1,1]{2,1,0:T(1,128)S(1)} async-done(((s32[128,1,1]{2,1,0:T(1,128)}), s32[128,1,1]{2,1,0:T(1,128)S(1)}, u32[]{:S(2)}, u32[]{:S(2)}) %all-to-all-start) | async-done | bytes 544 | tf_op jit(solution)/shard_map/all_to_all | solution.py:129
  48.5 5.6 all-to-all-start.2
  57.2 4.6 fusion.70
  61.7 7.5 all-to-all-done.2
  69.2 9.3 %all-to-all-start.1 = ((bf16[128,1,128,128]{3,2,1,0:T(8,128)(2,1)}), bf16[128,1,128,128]{3,2,1,0:T(8,128)(2,1)}, u32[]{:S(2)}, u32[]{:S(2)}) async-start(bf16[128,1,128,128]{3,2,1,0:T(8,128)(2,1)} %fusion.70), calls=%async_computation.1 | async-start | bytes 8388608 | tf_op jit(solution)/shard_map/all_to_all | solution.py:131
  79.7 182.3 %all-to-all-done.1 = bf16[128,1,128,128]{3,2,1,0:T(8,128)(2,1)} async-done(((bf16[128,1,128,128]{3,2,1,0:T(8,128)(2,1)}), bf16[128,1,128,128]{3,2,1,0:T(8,128)(2,1)}, u32[]{:S(2)}, u32[]{:S(2)}) %all-to-all-start.1) | async-done | bytes 4194336 | tf_op jit(solution)/shard_map/all_to_all | solution.py:131
  262.1 4.6 pad_maximum_fusion
  266.7 4.4 fusion.69
  271.2 45.2 %while.32 = (s32[]{:T(128)}, f32[6,2,128]{2,1,0:T(2,128)S(1)}, s32[6]{0:T(128)S(1)}, pred[12,16]{1,0:T(8,128)(4,1)S(1)}, f32[12,128]{1,0:T(8,128)S(1)}, /*index=...) while((s32[]{:T(128)}, f32[6,2,128]{2,1,0:T(2,128)S(1)}, ...), condition=%wide.region_5.10_spmd, body=%wide.region_3.9_spmd.sunk | while | flops 139474112 | bytes 3365755 | solution.py:61
  273.8 3.0 gather_fusion
  281.3 3.0 gather_fusion
  288.8 3.0 gather_fusion
  296.4 3.0 gather_fusion
  311.4 3.0 gather_fusion
  317.8 13.1 %all-to-all-start.3 = ((bf16[128,1,128]{2,1,0:T(2,128)(2,1)}), bf16[128,1,128]{2,1,0:T(2,128)(2,1)S(1)}, u32[]{:S(2)}, u32[]{:S(2)}) async-start(bf16[128,1,128]{2,1,0:T(2,128)(2,1)} %copy.71), calls=%async_computation.3 | async-start | bytes 131072 | tf_op jit(solution)/shard_map/all_to_all | solution.py:153
  330.9 14.8 %all-to-all-done.3 = bf16[128,1,128]{2,1,0:T(2,128)(2,1)S(1)} async-done(((bf16[128,1,128]{2,1,0:T(2,128)(2,1)}), bf16[128,1,128]{2,1,0:T(2,128)(2,1)S(1)}, u32[]{:S(2)}, u32[]{:S(2)}) %all-to-all-start.3) | async-done | bytes 32800 | tf_op jit(solution)/shard_map/all_to_all | solution.py:153
  345.7 5.9 all-to-all-start.4
  352.1 14.5 %all-to-all-done.4 = bf16[128,1,128]{2,1,0:T(2,128)(2,1)S(1)} async-done(((bf16[128,1,128]{2,1,0:T(2,128)(2,1)}), bf16[128,1,128]{2,1,0:T(2,128)(2,1)S(1)}, u32[]{:S(2)}, u32[]{:S(2)}) %all-to-all-start.4) | async-done | bytes 32800 | tf_op jit(solution)/shard_map/all_to_all | solution.py:137
  366.6 3.8 fusion.72
  372.1 69.3 %while.33 = (s32[]{:T(128)}, f32[6,2,128]{2,1,0:T(2,128)S(1)}, f32[6,2,64,128]{3,2,1,0:T(8,128)S(1)}, s32[6]{0:T(128)S(1)}, pred[12,16]{1,0:T(8,128)(4,1)S(1)}, ...) while((s32[]{:T(128)}, f32[6,2,128]{2,1,0:T(2,128)S(1)}, ...), condition=%wide.region_8.14_spmd, body=%wide.region_6.13_spmd.sunk | while | flops 208422080 | bytes 8232599 | solution.py:61
  386.9 3.0 gather_fusion.3
  398.4 3.0 gather_fusion.3
  441.9 100.7 %psum.14 = f32[64,64]{0,1:T(8,128)S(1)} all-reduce(f32[64,64]{0,1:T(8,128)S(1)} %convolution_bitcast_fusion.4), channel_id=1, replica_groups=mesh['rows'=128,'grp'=4] {'rows','grp'}, use_global_device_ids=true, to_apply=%region_9.15 | all-reduce | flops 4096 | bytes 32768 | tf_op jit(solution)/shard_map/psum | solution.py:90
  542.7 5.8 cholesky.44
  549.9 4.9 custom-call.6
  558.1 9.4 %all-to-all-start.5 = ((bf16[128,1,64,128]{3,2,1,0:T(8,128)(2,1)}), bf16[128,1,64,128]{3,2,1,0:T(8,128)(2,1)S(1)}, u32[]{:S(2)}, u32[]{:S(2)}) async-start(bf16[128,1,64,128]{3,2,1,0:T(8,128)(2,1)} %fusion.71), calls=%async_computation.5 | async-start | bytes 4194304 | tf_op jit(solution)/shard_map/all_to_all | solution.py:185
  570.5 93.9 %all-to-all-done.5 = bf16[128,1,64,128]{3,2,1,0:T(8,128)(2,1)S(1)} async-done(((bf16[128,1,64,128]{3,2,1,0:T(8,128)(2,1)}), bf16[128,1,64,128]{3,2,1,0:T(8,128)(2,1)S(1)}, u32[]{:S(2)}, u32[]{:S(2)}) %all-to-all-start.5) | async-done | bytes 2097184 | tf_op jit(solution)/shard_map/all_to_all | solution.py:185
  666.0 57.1 %while.34 = (s32[]{:T(128)}, f32[6,2,64,128]{3,2,1,0:T(8,128)S(1)}, s32[6]{0:T(128)S(1)}, s32[12,16]{1,0:T(8,128)S(1)}, bf16[140,64,128]{2,1,0:T(8,128)(2,1)}, /...) while((s32[]{:T(128)}, f32[6,2,64,128]{3,2,1,0:T(8,128)S(1)}, ...), condition=%wide.region_13.21_spmd, body=%wide.region_12.20_spmd.sunk | while | flops 206845376 | bytes 5001731 | solution.py:61
  723.6 101.9 %psum.15 = f32[64,64]{0,1:T(8,128)S(1)} all-reduce(f32[64,64]{0,1:T(8,128)S(1)} %convolution_bitcast_fusion.2), channel_id=1, replica_groups=mesh['rows'=128,'grp'=4] {'rows','grp'}, use_global_device_ids=true, to_apply=%region_14.22 | all-reduce | flops 4096 | bytes 32768 | tf_op jit(solution)/shard_map/psum | solution.py:90
  825.6 5.8 cholesky.55
  832.8 4.9 custom-call.7
  (341 shorter events, 173.3 us)
Async XLA Ops:
  0.6 351.1 %copy-start = (bf16[128,64]{0,1:T(8,128)(2,1)S(1)}, bf16[128,64]{0,1:T(8,128)(2,1)}, u32[]{:S(2)}) copy-start(bf16[128,64]{0,1:T(8,128)(2,1)} %param.30) | copy-start | bytes 49156
  0.6 53.5 %copy-start.1 = (bf16[1,1536,128]{2,1,0:T(8,128)(2,1)S(1)}, bf16[1,1536,128]{2,1,0:T(8,128)(2,1)}, u32[]{:S(2)}) copy-start(bf16[1,1536,128]{2,1,0:T(8,128)(2,1)} %param.25) | copy-start | bytes 1179652
  4.0 35.2 %all-to-all-start = ((s32[128,1,1]{2,1,0:T(1,128)}), s32[128,1,1]{2,1,0:T(1,128)S(1)}, u32[]{:S(2)}, u32[]{:S(2)}) async-start(s32[128,1,1]{2,1,0:T(1,128)} %copy.68), calls=%async_computation | async-start | bytes 131072 | tf_op jit(solution)/shard_map/all_to_all | solution.py:129
  48.5 20.7 %all-to-all-start.2 = ((bf16[128,1,128]{2,1,0:T(2,128)(2,1)}), bf16[128,1,128]{2,1,0:T(2,128)(2,1)S(1)}, u32[]{:S(2)}, u32[]{:S(2)}) async-start(bf16[128,1,128]{2,1,0:T(2,128)(2,1)} %copy.70), calls=%async_computation.2 | async-start | bytes 131072 | tf_op jit(solution)/shard_map/all_to_all | solution.py:134
  61.7 17.2 %copy-start.2 = (s32[1,12]{1,0:T(1,128)S(1)}, s32[1,12]{1,0:T(1,128)}, u32[]{:S(2)}) copy-start(s32[1,12]{1,0:T(1,128)} %param.29) | copy-start | bytes 148
  69.2 192.9 %all-to-all-start.1 = ((bf16[128,1,128,128]{3,2,1,0:T(8,128)(2,1)}), bf16[128,1,128,128]{3,2,1,0:T(8,128)(2,1)}, u32[]{:S(2)}, u32[]{:S(2)}) async-start(bf16[128,1,128,128]{3,2,1,0:T(8,128)(2,1)} %fusion.70), calls=%async_computation.1 | async-start | bytes 8388608 | tf_op jit(solution)/shard_map/all_to_all | solution.py:131
  317.8 28.0 %all-to-all-start.3 = ((bf16[128,1,128]{2,1,0:T(2,128)(2,1)}), bf16[128,1,128]{2,1,0:T(2,128)(2,1)S(1)}, u32[]{:S(2)}, u32[]{:S(2)}) async-start(bf16[128,1,128]{2,1,0:T(2,128)(2,1)} %copy.71), calls=%async_computation.3 | async-start | bytes 131072 | tf_op jit(solution)/shard_map/all_to_all | solution.py:153
  345.7 20.8 %all-to-all-start.4 = ((bf16[128,1,128]{2,1,0:T(2,128)(2,1)}), bf16[128,1,128]{2,1,0:T(2,128)(2,1)S(1)}, u32[]{:S(2)}, u32[]{:S(2)}) async-start(bf16[128,1,128]{2,1,0:T(2,128)(2,1)} %copy.72), calls=%async_computation.4 | async-start | bytes 131072 | tf_op jit(solution)/shard_map/all_to_all | solution.py:137
  558.1 106.2 %all-to-all-start.5 = ((bf16[128,1,64,128]{3,2,1,0:T(8,128)(2,1)}), bf16[128,1,64,128]{3,2,1,0:T(8,128)(2,1)S(1)}, u32[]{:S(2)}, u32[]{:S(2)}) async-start(bf16[128,1,64,128]{3,2,1,0:T(8,128)(2,1)} %fusion.71), calls=%async_computation.5 | async-start | bytes 4194304 | tf_op jit(solution)/shard_map/all_to_all | solution.py:185
where the time goes:
time: 850 us; the launch traced here: 839 us
  waiting for transfers between devices  326 us (38%)
  blocking collectives  203 us (24%)
  local copies, waits for them, and re-layouts  133 us (16%)
  starting transfers between devices  63.9 us (8%)
  other arithmetic  60.4 us (7%)
  matrix products  40 us (5%)
  loops' own time  11.9 us (1%)
    psum x2, blocking collectives, orthonormal(): gram_matrix = lax.psum(local_gram, ('rows', 'grp')) / total_rows  203 us
    all_to_all x1, waiting for transfers between devices, shards(): lax.all_to_all(jnp.take(own_rows, requested, axis=0), 'rows', split_axis=...  182 us
    gather x72, local copies, waits for them, and re-layouts, one_block(): gathered = [jnp.take(member, slot_block, axis=0) for member in pool_arrays]  107 us
    all_to_all x1, waiting for transfers between devices, shards(): lax.all_to_all(jnp.take(own_next, requested, axis=0), 'rows', split_axis=...  93.9 us
    dot_general x12, matrix products, kernel_tiles(): jnp.einsum('naf,nsbf->nsab', own_rows, part_rows, preferred_element_type=...  21.5 us
    all_to_all x1, starting transfers between devices, shards(): lax.all_to_all(wanted, 'rows', split_axis=0, concat_axis=0, tiled=True)  20.4 us
  transfers between devices with their start and end apart: 6, of which 6 were waited for; matrix products, arithmetic and copies ran while one was open for 2% of the time, Pallas kernels for 0%

commit v1 on v0

--- a/solution.py
+++ b/solution.py
@@ -87,7 +87,7 @@
 
 def orthonormal(raw_basis, total_rows):
     local_gram = jnp.einsum("nca,nda->cd", raw_basis, raw_basis, precision=lax.Precision.HIGHEST)
-    gram_matrix = lax.psum(local_gram, ("rows", "grp")) / total_rows
+    gram_matrix = jnp.sum(lax.all_gather(local_gram, ("rows", "grp")), 0) / total_rows
     lower = jnp.linalg.cholesky(gram_matrix)
     identity = jnp.eye(gram_matrix.shape[0], dtype=jnp.float32)
     lower_inverse = lax.linalg.triangular_solve(lower, identity, left_side=True, lower=True)

time: 850 us -> 1100 us (1.29)
  waiting for transfers between devices: 326 us -> 753 us
  blocking collectives: 203 us -> 0 us
  other arithmetic: 60.4 us -> 74.3 us
  between operations: 1.32 us -> 14.7 us
    all_gather x0 -> x2, waiting for transfers between devices: none -> 424 us  [orthonormal(): lax.all_gather(local_gram, ('rows', 'grp'))]
    psum x2 -> x0, blocking collectives: 203 us -> none  [orthonormal(): gram_matrix = lax.psum(local_gram, ('rows', 'grp')) / total_rows]
    reduce_sum x0 -> x2, other arithmetic: none -> 13.9 us  [orthonormal(): jnp.sum(lax.all_gather(local_gram, ('rows', 'grp')), 0) / total_rows]
  transfers between devices with their start and end apart: 6 -> 8, of which waited for: 6 -> 8; matrix products, arithmetic and copies ran while one was open for 2% -> 1% of each run, Pallas kernels for 0% -> 0%
where the time goes in v1:
time: 1100 us; the launch traced here: 1090 us
  waiting for transfers between devices  753 us (68%)
  local copies, waits for them, and re-layouts  132 us (12%)
  other arithmetic  74.3 us (7%)
  starting transfers between devices  66.1 us (6%)
  matrix products  41.1 us (4%)
  between operations  14.7 us (1%)
  loops' own time  12.8 us (1%)
    all_gather x2, waiting for transfers between devices, orthonormal(): lax.all_gather(local_gram, ('rows', 'grp'))  424 us
    all_to_all x1, waiting for transfers between devices, shards(): lax.all_to_all(jnp.take(own_rows, requested, axis=0), 'rows', split_axis=...  182 us
    gather x72, local copies, waits for them, and re-layouts, one_block(): gathered = [jnp.take(member, slot_block, axis=0) for member in pool_arrays]  107 us
    all_to_all x1, waiting for transfers between devices, shards(): lax.all_to_all(jnp.take(own_next, requested, axis=0), 'rows', split_axis=...  96.6 us
  transfers between devices with their start and end apart: 8, of which 8 were waited for; matrix products, arithmetic and copies ran while one was open for 1% of the time, Pallas kernels for 0%

profile of v1, /device:TPU:1, one launch (start us, length us, event | category | flops | bytes accessed | tf_op | source)
XLA Modules:
  0.0 1093.8 jit_solution(13079601982143777893)
XLA Ops:
  10.5 20.4 %all-to-all-start = ((s32[128,1,1]{2,1,0:T(1,128)}), s32[128,1,1]{2,1,0:T(1,128)S(1)}, u32[]{:S(2)}, u32[]{:S(2)}) async-start(s32[128,1,1]{2,1,0:T(1,128)} %copy.64), calls=%async_computation | async-start | bytes 131072 | tf_op jit(solution)/shard_map/all_to_all | solution.py:129
  32.4 13.4 %all-to-all-done = s32[128,1,1]{2,1,0:T(1,128)S(1)} async-done(((s32[128,1,1]{2,1,0:T(1,128)}), s32[128,1,1]{2,1,0:T(1,128)S(1)}, u32[]{:S(2)}, u32[]{:S(2)}) %all-to-all-start) | async-done | bytes 544 | tf_op jit(solution)/shard_map/all_to_all | solution.py:129
  55.0 5.6 all-to-all-start.2
  60.7 3.1 gather_fusion.12
  63.8 4.6 fusion.70
  68.4 7.4 all-to-all-done.2
  75.8 9.9 all-to-all-start.1
  86.8 182.3 %all-to-all-done.1 = bf16[128,1,128,128]{3,2,1,0:T(8,128)(2,1)} async-done(((bf16[128,1,128,128]{3,2,1,0:T(8,128)(2,1)}), bf16[128,1,128,128]{3,2,1,0:T(8,128)(2,1)}, u32[]{:S(2)}, u32[]{:S(2)}) %all-to-all-start.1) | async-done | bytes 4194336 | tf_op jit(solution)/shard_map/all_to_all | solution.py:131
  269.2 4.6 pad_maximum_fusion
  273.8 4.4 fusion.69
  278.3 45.6 %while.32 = (s32[]{:T(128)}, f32[6,2,128]{2,1,0:T(2,128)S(1)}, s32[6]{0:T(128)S(1)}, pred[12,16]{1,0:T(8,128)(4,1)S(1)}, f32[12,128]{1,0:T(8,128)S(1)}, /*index=...) while((s32[]{:T(128)}, f32[6,2,128]{2,1,0:T(2,128)S(1)}, ...), condition=%wide.region_5.10_spmd, body=%wide.region_3.9_spmd.sunk | while | flops 139474112 | bytes 3365755 | solution.py:61
  280.9 3.0 gather_fusion
  303.7 3.0 gather_fusion
  311.3 3.0 gather_fusion
  318.9 3.0 gather_fusion
  325.3 13.1 %all-to-all-start.3 = ((bf16[128,1,128]{2,1,0:T(2,128)(2,1)}), bf16[128,1,128]{2,1,0:T(2,128)(2,1)S(1)}, u32[]{:S(2)}, u32[]{:S(2)}) async-start(bf16[128,1,128]{2,1,0:T(2,128)(2,1)} %copy.67), calls=%async_computation.3 | async-start | bytes 131072 | tf_op jit(solution)/shard_map/all_to_all | solution.py:153
  338.5 14.8 %all-to-all-done.3 = bf16[128,1,128]{2,1,0:T(2,128)(2,1)S(1)} async-done(((bf16[128,1,128]{2,1,0:T(2,128)(2,1)}), bf16[128,1,128]{2,1,0:T(2,128)(2,1)S(1)}, u32[]{:S(2)}, u32[]{:S(2)}) %all-to-all-start.3) | async-done | bytes 32800 | tf_op jit(solution)/shard_map/all_to_all | solution.py:153
  353.3 5.6 all-to-all-start.4
  359.5 14.5 %all-to-all-done.4 = bf16[128,1,128]{2,1,0:T(2,128)(2,1)S(1)} async-done(((bf16[128,1,128]{2,1,0:T(2,128)(2,1)}), bf16[128,1,128]{2,1,0:T(2,128)(2,1)S(1)}, u32[]{:S(2)}, u32[]{:S(2)}) %all-to-all-start.4) | async-done | bytes 32800 | tf_op jit(solution)/shard_map/all_to_all | solution.py:137
  374.1 3.8 fusion.72
  379.5 69.3 %while.33 = (s32[]{:T(128)}, f32[6,2,128]{2,1,0:T(2,128)S(1)}, f32[6,2,64,128]{3,2,1,0:T(8,128)S(1)}, s32[6]{0:T(128)S(1)}, pred[12,16]{1,0:T(8,128)(4,1)S(1)}, ...) while((s32[]{:T(128)}, f32[6,2,128]{2,1,0:T(2,128)S(1)}, ...), condition=%wide.region_8.14_spmd, body=%wide.region_6.13_spmd.sunk | while | flops 208422080 | bytes 8232599 | solution.py:61
  449.9 210.7 %all-gather.5.cloned.1.call-done = f32[32768,64]{1,0:T(8,128)} async-done(((f32[64,64]{1,0:T(8,128)}), f32[32768,64]{1,0:T(8,128)}) %all-gather.5.cloned.1.call-update) | async-done | bytes 8388624 | tf_op jit(solution)/shard_map/all_gather | solution.py:90
  660.6 6.9 reduce_sum.52
  667.8 5.8 cholesky.44
  674.9 4.9 custom-call.6
  683.2 10.9 all-to-all-start.5
  694.4 96.6 %all-to-all-done.5 = bf16[128,1,64,128]{3,2,1,0:T(8,128)(2,1)S(1)} async-done(((bf16[128,1,64,128]{3,2,1,0:T(8,128)(2,1)}), bf16[128,1,64,128]{3,2,1,0:T(8,128)(2,1)S(1)}, u32[]{:S(2)}, u32[]{:S(2)}) %all-to-all-start.5) | async-done | bytes 2097184 | tf_op jit(solution)/shard_map/all_to_all | solution.py:185
  792.6 57.7 %while.34 = (s32[]{:T(128)}, f32[6,2,64,128]{3,2,1,0:T(8,128)S(1)}, s32[6]{0:T(128)S(1)}, s32[12,16]{1,0:T(8,128)S(1)}, bf16[140,64,128]{2,1,0:T(8,128)(2,1)}, /...) while((s32[]{:T(128)}, f32[6,2,64,128]{3,2,1,0:T(8,128)S(1)}, ...), condition=%wide.region_13.21_spmd, body=%wide.region_12.20_spmd.sunk | while | flops 206845376 | bytes 5001731 | solution.py:61
  852.5 213.5 %all-gather.7.cloned.1.call-done = f32[32768,64]{1,0:T(8,128)} async-done(((f32[64,64]{1,0:T(8,128)}), f32[32768,64]{1,0:T(8,128)}) %all-gather.7.cloned.1.call-update) | async-done | bytes 8388624 | tf_op jit(solution)/shard_map/all_gather | solution.py:90
  1066.0 6.9 reduce_sum.53
  1073.1 5.8 cholesky.55
  1080.3 4.9 custom-call.7
  (351 shorter events, 179.5 us)
Async XLA Ops:
  7.2 352.0 %copy-start = (bf16[128,64]{0,1:T(8,128)(2,1)S(1)}, bf16[128,64]{0,1:T(8,128)(2,1)}, u32[]{:S(2)}) copy-start(bf16[128,64]{0,1:T(8,128)(2,1)} %param.30) | copy-start | bytes 49156
  7.2 53.5 %copy-start.2 = (bf16[1,1536,128]{2,1,0:T(8,128)(2,1)S(1)}, bf16[1,1536,128]{2,1,0:T(8,128)(2,1)}, u32[]{:S(2)}) copy-start(bf16[1,1536,128]{2,1,0:T(8,128)(2,1)} %param.25) | copy-start | bytes 1179652
  10.5 35.2 %all-to-all-start = ((s32[128,1,1]{2,1,0:T(1,128)}), s32[128,1,1]{2,1,0:T(1,128)S(1)}, u32[]{:S(2)}, u32[]{:S(2)}) async-start(s32[128,1,1]{2,1,0:T(1,128)} %copy.64), calls=%async_computation | async-start | bytes 131072 | tf_op jit(solution)/shard_map/all_to_all | solution.py:129
  55.0 20.7 %all-to-all-start.2 = ((bf16[128,1,128]{2,1,0:T(2,128)(2,1)}), bf16[128,1,128]{2,1,0:T(2,128)(2,1)S(1)}, u32[]{:S(2)}, u32[]{:S(2)}) async-start(bf16[128,1,128]{2,1,0:T(2,128)(2,1)} %copy.66), calls=%async_computation.2 | async-start | bytes 131072 | tf_op jit(solution)/shard_map/all_to_all | solution.py:134
  68.4 17.7 %copy-start.3 = (s32[1,12]{1,0:T(1,128)S(1)}, s32[1,12]{1,0:T(1,128)}, u32[]{:S(2)}) copy-start(s32[1,12]{1,0:T(1,128)} %param.29) | copy-start | bytes 148
  75.8 193.4 %all-to-all-start.1 = ((bf16[128,1,128,128]{3,2,1,0:T(8,128)(2,1)}), bf16[128,1,128,128]{3,2,1,0:T(8,128)(2,1)}, u32[]{:S(2)}, u32[]{:S(2)}) async-start(bf16[128,1,128,128]{3,2,1,0:T(8,128)(2,1)} %fusion.70), calls=%async_computation.1 | async-start | bytes 8388608 | tf_op jit(solution)/shard_map/all_to_all | solution.py:131
  325.3 28.0 %all-to-all-start.3 = ((bf16[128,1,128]{2,1,0:T(2,128)(2,1)}), bf16[128,1,128]{2,1,0:T(2,128)(2,1)S(1)}, u32[]{:S(2)}, u32[]{:S(2)}) async-start(bf16[128,1,128]{2,1,0:T(2,128)(2,1)} %copy.67), calls=%async_computation.3 | async-start | bytes 131072 | tf_op jit(solution)/shard_map/all_to_all | solution.py:153
  353.3 20.7 %all-to-all-start.4 = ((bf16[128,1,128]{2,1,0:T(2,128)(2,1)}), bf16[128,1,128]{2,1,0:T(2,128)(2,1)S(1)}, u32[]{:S(2)}, u32[]{:S(2)}) async-start(bf16[128,1,128]{2,1,0:T(2,128)(2,1)} %copy.68), calls=%async_computation.4 | async-start | bytes 131072 | tf_op jit(solution)/shard_map/all_to_all | solution.py:137
  358.9 301.7 %all-gather.5.cloned.1.call-start = ((), (), s32[]{:S(2)}) async-start(), calls=%async_computation.6 | async-start | bytes 16809984 | tf_op jit(solution)/shard_map/all_gather | solution.py:90
  683.2 107.8 %all-to-all-start.5 = ((bf16[128,1,64,128]{3,2,1,0:T(8,128)(2,1)}), bf16[128,1,64,128]{3,2,1,0:T(8,128)(2,1)S(1)}, u32[]{:S(2)}, u32[]{:S(2)}) async-start(bf16[128,1,64,128]{3,2,1,0:T(8,128)(2,1)} %fusion.71), calls=%async_computation.5 | async-start | bytes 4194304 | tf_op jit(solution)/shard_map/all_to_all | solution.py:185
  694.1 371.9 %all-gather.7.cloned.1.call-start = ((), (), s32[]{:S(2)}) async-start(), calls=%async_computation.7 | async-start | bytes 16809984 | tf_op jit(solution)/shard_map/all_gather | solution.py:90
  1066.0 20.7 %copy-start.1 = (bf16[128,64]{0,1:T(8,128)(2,1)S(1)}, bf16[128,64]{0,1:T(8,128)(2,1)}, u32[]{:S(2)}) copy-start(bf16[128,64]{0,1:T(8,128)(2,1)} %param.30) | copy-start | bytes 49156
Sparse Core Ops, SparseCore 0:
  450.1 210.5 all-gather.4
  851.6 214.3 all-gather.6
